TPU v7x, 32 devices: a whole 2x2x4 slice. The times are simulated.
32 devices in a mesh: grp: 2 (over y), dp: 16 (over z, x, core).
Axes of the slice: x: 2, y: 2, z: 4, core: 2. Of those that a mesh axis runs over, the one named last changes fastest.
Arguments:
- query_act: bfloat16 [32768, 256], P(('grp', 'dp')), parts along dimension 0, may hold values from -6 to 6
- query_grad: bfloat16 [32768, 256], P(('grp', 'dp')), parts along dimension 0, may hold values from -6 to 6
- train_act: bfloat16 [32, 64, 256], P(('grp', 'dp')), parts along dimension 0, may hold values from -12 to 12
- train_grad: bfloat16 [32, 64, 256], P(('grp', 'dp')), parts along dimension 0, may hold values from -12 to 12
- seq_ids: int32 [32, 64], P(('grp', 'dp')), parts along dimension 0, may hold values from 0 to 3, never falling along the last dimension, each value on 1 to 32 neighbouring positions
Outputs:
- scores: float32 [32768, 64], P(('grp', 'dp')), parts along dimension 0
There are 2 independent parts, one for each index of `grp`. A program takes and returns all parts, laid end to end along the dimension named above; each array names one. Nothing has to cross between parts.
Inputs may be any that keep to these rules, and one draw needn't show every extreme that they name: `seq_ids`: within a span the ids never fall and each of the 4 sequences holds 1 to 32 tokens, one exactly 32.
All inputs are finite; a program needn't handle non-finite values.
Results may differ from a plain program's by a relative error of at most 0.023.
The roundings to bfloat16 on the way count: a program that leaves them out, or rounds other values in their place, can miss the bound.
Values may be sent and summed in bfloat16 or wider, within the bound.
No kernel may reach another device: no remote copies, remote signals or barrier semaphores. Data moves between devices by JAX's collectives and lax.ppermute only.
A program may use at most 192 MiB of HBM per device.

v0:
```python
import math

import jax
import jax.numpy as jnp
from jax import lax
from jax.experimental import pallas as pl
from jax.experimental.pallas import tpu as pltpu
from jax.sharding import PartitionSpec as P

SEQ_DEV = 4
DAMPING = 0.1

BF16 = jnp.bfloat16
F32 = jnp.float32


def newton_schedule():
    radius, bounds, scales = 3e-3, [], []
    for _ in range(13):
        before = math.sqrt(2.0 * radius / (1.0 + radius))
        scales.append(2.0 / (2.0 - before * before))
        bounds.append(2.0 * DAMPING / (1.0 - before) - DAMPING)
        radius = before
    return bounds, scales


BOUNDS, SCALES = newton_schedule()


def pick(index, values):
    out = jnp.float32(values[0])
    for position, value in enumerate(values[1:], 2):
        out = jnp.where(index == position, jnp.float32(value), out)
    return out


def split2(x):
    high = x.astype(BF16)
    return high, (x - high.astype(F32)).astype(BF16)


def split3(x):
    high = x.astype(BF16)
    rest = x - high.astype(F32)
    mid = rest.astype(BF16)
    return high, mid, (rest - mid.astype(F32)).astype(BF16)


def dot(a, b):
    return jnp.dot(a, b, preferred_element_type=F32)


def dot3(a, b):
    return dot(a[0], b[0]) + (dot(a[0], b[1]) + dot(a[1], b[0]))


def dot6(a, b):
    small = dot(a[1], b[1]) + (dot(a[0], b[2]) + dot(a[2], b[0]))
    return dot(a[0], b[0]) + ((dot(a[0], b[1]) + dot(a[1], b[0])) + small)


def dot_nt(a, b):
    return lax.dot_general(a, b, (((1,), (1,)), ((), ())), preferred_element_type=F32)


def influence_kernel(rows, scale, *refs):
    n_pieces = len(refs) - 10
    pieces = refs[:n_pieces]
    query_act, query_grad, out, act, grad, onehot, mat, tmat, xmat, inverse = refs[n_pieces:]
    tokens, width = act.shape
    columns = onehot.shape[0]
    lane = lax.broadcasted_iota(jnp.int32, (1, 128), 1)
    column = lax.broadcasted_iota(jnp.int32, (columns, 128), 0)

    spans = [(ref, k) for ref in pieces for k in range(ref.shape[0])]
    labels = []
    for slot, (ref, k) in enumerate(spans):
        act[slot * rows : (slot + 1) * rows, :] = ref[k, 0:rows, :]
        grad[slot * rows : (slot + 1) * rows, :] = ref[k, rows : 2 * rows, :]
        tail = ref[k, 2 * rows : 2 * rows + 16, 0:128].astype(F32)
        labels.append((SEQ_DEV * tail[1:2, :] + tail[0:1, :]).astype(jnp.int32))
    for pair in range(tokens // 128):
        label = jnp.where(lane < rows, labels[2 * pair], labels[2 * pair + 1])
        onehot[:, pair * 128 : (pair + 1) * 128] = (column == label).astype(F32).astype(BF16)

    diagonal = lax.broadcasted_iota(jnp.int32, (width, width), 0) == lax.broadcasted_iota(jnp.int32, (width, width), 1)
    eye = diagonal.astype(F32)
    norm = jnp.float32(0.0)
    for which, features in enumerate((act, grad)):
        flat = features[...]
        covar = lax.dot_general(flat, flat, (((0,), (0,)), ((), ())), preferred_element_type=F32)
        matrix = covar * (1.0 / tokens) + DAMPING * eye
        mat[which] = matrix
        norm = jnp.maximum(norm, jnp.sum(matrix * matrix))

    steps = jnp.int32(2)
    for bound in BOUNDS[1:-1]:
        steps = steps + (norm > bound * bound).astype(jnp.int32)
    start = pick(steps, [2.0 / (DAMPING + bound) for bound in BOUNDS])

    first = pick(steps, SCALES)
    for which in range(2):
        t = start * mat[which]
        parts = split2(t)
        xmat[which] = (first * start) * (2.0 * eye - t)
        tmat[which] = first * (2.0 * t - dot3(parts, parts))

    def step(i, carry):
        factor = pick(steps - i, SCALES)
        for which in range(2):
            t, x = tmat[which], xmat[which]
            tparts, xparts = split2(t), split2(x)
            xmat[which] = factor * (2.0 * x - dot3(xparts, tparts))
            tmat[which] = factor * (2.0 * t - dot3(tparts, tparts))
        return carry

    lax.fori_loop(1, steps - 1, step, 0)
    for which in range(2):
        t, x = tmat[which], xmat[which]
        xmat[which] = SCALES[0] * (2.0 * x - dot3(split2(x), split2(t)))

    def correct(i, carry):
        for which in range(2):
            x = xmat[which]
            xparts = split3(x)
            residual = eye - dot6(split3(mat[which]), xparts)
            xmat[which] = x + dot3(xparts, split2(residual))
        return carry

    lax.fori_loop(0, jnp.maximum(steps - 8, 0) + 1, correct, 0)
    for which in range(2):
        high, mid = split2(xmat[which])
        inverse[2 * which] = high
        inverse[2 * which + 1] = mid

    block, chunk = 256, min(tokens, 1024)

    def scores(i, carry):
        here = pl.ds(pl.multiple_of(i * block, block), block)
        qa, qg = query_act[here, :], query_grad[here, :]
        pa = (dot(qa, inverse[0]) + dot(qa, inverse[1])).astype(BF16)
        pg = (dot(qg, inverse[2]) + dot(qg, inverse[3])).astype(BF16)
        total = jnp.zeros((block, columns), F32)
        for first_token in range(0, tokens, chunk):
            these = slice(first_token, first_token + chunk)
            product = dot_nt(pa, act[these, :]) * dot_nt(pg, grad[these, :])
            high, mid = split2(product)
            selector = onehot[:, these]
            total = total + (dot_nt(high, selector) + dot_nt(mid, selector))
        out[here, :] = total * scale
        return carry

    lax.fori_loop(0, query_act.shape[0] // block, scores, 0, unroll=tokens <= 1024)


def gather_spans(payload, size):
    held = [payload]
    bits = [1 << k for k in range(size.bit_length() - 1)]
    for bit in reversed(bits):
        if len(held) >= 16:
            held = [jnp.concatenate(held, axis=0)]
        pairs = [(device, device ^ bit) for device in range(size)]
        held = held + [lax.ppermute(piece, "dp", pairs) for piece in held]
    return held


def local(query_act, query_grad, train_act, train_grad, seq_ids):
    size = lax.axis_size("dp")
    spans, rows, width = train_act.shape
    own = lax.axis_index("dp").astype(BF16)
    ids = jnp.tile(seq_ids.astype(BF16), (1, width // rows)).reshape(spans, 1, width)
    index = jnp.full((spans, 15, width), own, BF16)
    payload = jnp.concatenate([train_act, train_grad, ids, index], axis=1)
    pieces = gather_spans(payload, size)
    tokens, queries, columns = size * spans * rows, query_act.shape[0], size * spans * SEQ_DEV
    scale = 1.0 / (8.0 * math.sqrt(query_act.shape[1] * query_grad.shape[1]))
    vmem = pl.BlockSpec(memory_space=pltpu.VMEM)

    def kernel(*refs):
        influence_kernel(rows, scale, *refs)

    return pl.pallas_call(
        kernel,
        out_shape=jax.ShapeDtypeStruct((queries, columns), F32),
        in_specs=[vmem] * (len(pieces) + 2),
        out_specs=vmem,
        scratch_shapes=[
            pltpu.VMEM((tokens, width), BF16),
            pltpu.VMEM((tokens, width), BF16),
            pltpu.VMEM((columns, tokens), BF16),
            pltpu.VMEM((2, width, width), F32),
            pltpu.VMEM((2, width, width), F32),
            pltpu.VMEM((2, width, width), F32),
            pltpu.VMEM((4, width, width), BF16),
        ],
        compiler_params=pltpu.CompilerParams(vmem_limit_bytes=56 << 20),
    )(*pieces, query_act, query_grad)


def solution(mesh):
    in_specs = (
        P(("grp", "dp"), None),
        P(("grp", "dp"), None),
        P(("grp", "dp"), None, None),
        P(("grp", "dp"), None, None),
        P(("grp", "dp"), None),
    )
    out_specs = P(("grp", "dp"), None)
    return jax.shard_map(local, mesh=mesh, in_specs=in_specs, out_specs=out_specs, check_vma=False)
```

profile of v0, /device:TPU:0, one launch (start us, length us, event | category | flops | bytes accessed | tf_op | source)
XLA Modules:
  0.0 35.9 jit_solution(189250225601460161)
XLA Ops:
  0.0 0.7 %copy-done.16 = s32[1,64]{1,0:T(1,128)S(1)} copy-done((s32[1,64]{1,0:T(1,128)S(1)}, s32[1,64]{1,0:T(1,128)}, u32[]{:S(2)}) %copy-start.16) | copy-done | bytes 280
  0.7 0.1 tile.12
  0.8 0.1 pad.3.clone
  0.8 0.9 %maximum_maximum_fusion.refs_0_ = bf16[1,144,256]{2,1,0:T(8,128)(2,1)S(1)} fusion(bf16[1,1,256]{2,1,0:T(2,128)(2,1)S(1)} %tile.12, bf16[1,64,256]{2,1,0:T(8,128)(2,1)} %param.8, bf16[1,64,256]{2,1,0:T(8,128)(2,1)} %param.7, bf16[144]{0:T(256)(128)(2,1)S(1)} %pad.3.clone), kind=kLoop, calls=%fused_computation | loop fusion | flops 294912 | bytes 140064 | tf_op jit(solution)/shard_map/concatenate | solution.py:173
  1.7 0.0 copy-start
  1.7 4.1 %collective-permute-start = (bf16[1,144,256]{2,1,0:T(8,128)(2,1)S(1)}, bf16[1,144,256]{2,1,0:T(8,128)(2,1)S(1)}, u32[]{:S(2)}, u32[]{:S(2)}) collective-permute-start(bf16[1,144,256]{2,1,0:T(8,128)(2,1)S(1)} %maximum_maximum_fusion.refs_0_), channel_id=1, source_target_pairs={{0,8},{1,9},{2,10},{3,11},{4,12},{5,13},{6,14},{7,15},{8,0},{9,1},... | collective-permute-start | bytes 221192 | tf_op jit(solution)/shard_map/ppermute | solution.py:163
  5.8 1.5 %collective-permute-start.3 = (bf16[1,144,256]{2,1,0:T(8,128)(2,1)S(1)}, bf16[1,144,256]{2,1,0:T(8,128)(2,1)S(1)}, u32[]{:S(2)}, u32[]{:S(2)}) collective-permute-start(bf16[1,144,256]{2,1,0:T(8,128)(2,1)S(1)} %maximum_maximum_fusion.refs_0_), channel_id=1, source_target_pairs={{0,2},{1,3},{2,0},{3,1},{4,6},{5,7},{6,4},{7,5},{8,10},{9,11},{10,... | collective-permute-start | bytes 221192 | tf_op jit(solution)/shard_map/ppermute | solution.py:163
  7.3 1.6 %collective-permute-start.1 = (bf16[1,144,256]{2,1,0:T(8,128)(2,1)S(1)}, bf16[1,144,256]{2,1,0:T(8,128)(2,1)S(1)}, u32[]{:S(2)}, u32[]{:S(2)}) collective-permute-start(bf16[1,144,256]{2,1,0:T(8,128)(2,1)S(1)} %maximum_maximum_fusion.refs_0_), channel_id=1, source_target_pairs={{0,4},{1,5},{2,6},{3,7},{4,0},{5,1},{6,2},{7,3},{8,12},{9,13},{10,... | collective-permute-start | bytes 221192 | tf_op jit(solution)/shard_map/ppermute | solution.py:163
  8.9 0.6 %collective-permute-done.refs_1_ = bf16[1,144,256]{2,1,0:T(8,128)(2,1)S(1)} collective-permute-done((bf16[1,144,256]{2,1,0:T(8,128)(2,1)S(1)}, bf16[1,144,256]{2,1,0:T(8,128)(2,1)S(1)}, u32[]{:S(2)}, u32[]{:S(2)}) %collective-permute-start) | collective-permute-done | bytes 73760 | tf_op jit(solution)/shard_map/ppermute | solution.py:163
  9.4 1.1 %collective-permute-start.2 = (bf16[1,144,256]{2,1,0:T(8,128)(2,1)S(1)}, bf16[1,144,256]{2,1,0:T(8,128)(2,1)S(1)}, u32[]{:S(2)}, u32[]{:S(2)}) collective-permute-start(bf16[1,144,256]{2,1,0:T(8,128)(2,1)S(1)} %collective-permute-done.refs_1_), channel_id=1, source_target_pairs={{0,4},{1,5},{2,6},{3,7},{4,0},{5,1},{6,2},{7,3},{8,12},{9,13},{10,... | collective-permute-start | bytes 221192 | tf_op jit(solution)/shard_map/ppermute | solution.py:163
  10.6 1.1 %collective-permute-done.1.refs_2_ = bf16[1,144,256]{2,1,0:T(8,128)(2,1)S(1)} collective-permute-done((bf16[1,144,256]{2,1,0:T(8,128)(2,1)S(1)}, bf16[1,144,256]{2,1,0:T(8,128)(2,1)S(1)}, u32[]{:S(2)}, u32[]{:S(2)}) %collective-permute-start.1) | collective-permute-done | bytes 73760 | tf_op jit(solution)/shard_map/ppermute | solution.py:163
  11.7 0.8 %collective-permute-start.5 = (bf16[1,144,256]{2,1,0:T(8,128)(2,1)S(1)}, bf16[1,144,256]{2,1,0:T(8,128)(2,1)S(1)}, u32[]{:S(2)}, u32[]{:S(2)}) collective-permute-start(bf16[1,144,256]{2,1,0:T(8,128)(2,1)S(1)} %collective-permute-done.1.refs_2_), channel_id=1, source_target_pairs={{0,2},{1,3},{2,0},{3,1},{4,6},{5,7},{6,4},{7,5},{8,10},{9,11},{10,... | collective-permute-start | bytes 221192 | tf_op jit(solution)/shard_map/ppermute | solution.py:163
  12.5 1.2 %collective-permute-start.4 = (bf16[1,144,256]{2,1,0:T(8,128)(2,1)S(1)}, bf16[1,144,256]{2,1,0:T(8,128)(2,1)S(1)}, u32[]{:S(2)}, u32[]{:S(2)}) collective-permute-start(bf16[1,144,256]{2,1,0:T(8,128)(2,1)S(1)} %collective-permute-done.refs_1_), channel_id=1, source_target_pairs={{0,2},{1,3},{2,0},{3,1},{4,6},{5,7},{6,4},{7,5},{8,10},{9,11},{10,... | collective-permute-start | bytes 221192 | tf_op jit(solution)/shard_map/ppermute | solution.py:163
  13.7 0.1 collective-permute-done.2.refs_3_
  13.8 1.6 %collective-permute-start.6 = (bf16[1,144,256]{2,1,0:T(8,128)(2,1)S(1)}, bf16[1,144,256]{2,1,0:T(8,128)(2,1)S(1)}, u32[]{:S(2)}, u32[]{:S(2)}) collective-permute-start(bf16[1,144,256]{2,1,0:T(8,128)(2,1)S(1)} %collective-permute-done.2.refs_3_), channel_id=1, source_target_pairs={{0,2},{1,3},{2,0},{3,1},{4,6},{5,7},{6,4},{7,5},{8,10},{9,11},{10,... | collective-permute-start | bytes 221192 | tf_op jit(solution)/shard_map/ppermute | solution.py:163
  15.5 0.5 %collective-permute-start.10 = (bf16[1,144,256]{2,1,0:T(8,128)(2,1)S(1)}, bf16[1,144,256]{2,1,0:T(8,128)(2,1)S(1)}, u32[]{:S(2)}, u32[]{:S(2)}) collective-permute-start(bf16[1,144,256]{2,1,0:T(8,128)(2,1)S(1)} %collective-permute-done.2.refs_3_), channel_id=1, source_target_pairs={{0,1},{1,0},{2,3},{3,2},{4,5},{5,4},{6,7},{7,6},{8,9},{9,8},{10,11... | collective-permute-start | bytes 221192 | tf_op jit(solution)/shard_map/ppermute | solution.py:163
  15.9 0.8 %collective-permute-done.5.refs_6_ = bf16[1,144,256]{2,1,0:T(8,128)(2,1)S(1)} collective-permute-done((bf16[1,144,256]{2,1,0:T(8,128)(2,1)S(1)}, bf16[1,144,256]{2,1,0:T(8,128)(2,1)S(1)}, u32[]{:S(2)}, u32[]{:S(2)}) %collective-permute-start.5) | collective-permute-done | bytes 73760 | tf_op jit(solution)/shard_map/ppermute | solution.py:163
  16.7 1.6 %collective-permute-done.4.refs_5_ = bf16[1,144,256]{2,1,0:T(8,128)(2,1)S(1)} collective-permute-done((bf16[1,144,256]{2,1,0:T(8,128)(2,1)S(1)}, bf16[1,144,256]{2,1,0:T(8,128)(2,1)S(1)}, u32[]{:S(2)}, u32[]{:S(2)}) %collective-permute-start.4) | collective-permute-done | bytes 73760 | tf_op jit(solution)/shard_map/ppermute | solution.py:163
  18.3 1.2 %collective-permute-done.6.refs_7_ = bf16[1,144,256]{2,1,0:T(8,128)(2,1)S(1)} collective-permute-done((bf16[1,144,256]{2,1,0:T(8,128)(2,1)S(1)}, bf16[1,144,256]{2,1,0:T(8,128)(2,1)S(1)}, u32[]{:S(2)}, u32[]{:S(2)}) %collective-permute-start.6) | collective-permute-done | bytes 73760 | tf_op jit(solution)/shard_map/ppermute | solution.py:163
  19.6 0.0 collective-permute-done.12.refs_13_
  19.6 1.2 %collective-permute-done.14.refs_15_ = bf16[1,144,256]{2,1,0:T(8,128)(2,1)S(1)} collective-permute-done((bf16[1,144,256]{2,1,0:T(8,128)(2,1)S(1)}, bf16[1,144,256]{2,1,0:T(8,128)(2,1)S(1)}, u32[]{:S(2)}, u32[]{:S(2)}) %collective-permute-start.14) | collective-permute-done | bytes 73760 | tf_op jit(solution)/shard_map/ppermute | solution.py:163
  20.9 0.6 %copy-done.15 = bf16[1,144,256]{2,1,0:T(8,128)(2,1)} copy-done((bf16[1,144,256]{2,1,0:T(8,128)(2,1)}, bf16[1,144,256]{2,1,0:T(8,128)(2,1)S(1)}, u32[]{:S(2)}) %copy-start.15) | copy-done | bytes 73752
  21.5 12.4 %shard_map.55 = f32[1024,64]{1,0:T(8,128)} custom-call(bf16[1,144,256]{2,1,0:T(8,128)(2,1)} %copy-done, bf16[1,144,256]{2,1,0:T(8,128)(2,1)} %copy-done.1, bf16[1,144,256]{2,1,0:T(8,128)(2,1)} %copy-done.3, bf16[1,144,256]{2,1,0:T(8,128)(2,1)} %copy-done.5, bf16[1,144,256]{2,1,0:T(8,128)(2,1)} %copy-done.2, bf16[1,144,256]{2,1,0:T(8,128)(2,1)} %copy-done.9, ...), custom_call_target="tpu_custom_call" | custom-call | tf_op jit(solution)/shard_map/pallas_call | solution.py:182
  33.9 1.9 %copy.6 = f32[1024,64]{0,1:T(8,128)} copy(f32[1024,64]{1,0:T(8,128)} %shard_map.55) | data formatting | bytes 524288 | tf_op jit(solution)/shard_map/pallas_call | solution.py:182
  (48 shorter events, 0.1 us)
Async XLA Ops:
  1.7 19.1 %copy-start = (bf16[1,144,256]{2,1,0:T(8,128)(2,1)}, bf16[1,144,256]{2,1,0:T(8,128)(2,1)S(1)}, u32[]{:S(2)}) copy-start(bf16[1,144,256]{2,1,0:T(8,128)(2,1)S(1)} %maximum_maximum_fusion.refs_0_) | copy-start | bytes 221188
  1.7 7.7 %collective-permute-start = (bf16[1,144,256]{2,1,0:T(8,128)(2,1)S(1)}, bf16[1,144,256]{2,1,0:T(8,128)(2,1)S(1)}, u32[]{:S(2)}, u32[]{:S(2)}) collective-permute-start(bf16[1,144,256]{2,1,0:T(8,128)(2,1)S(1)} %maximum_maximum_fusion.refs_0_), channel_id=1, source_target_pairs={{0,8},{1,9},{2,10},{3,11},{4,12},{5,13},{6,14},{7,15},{8,0},{9,1},... | collective-permute-start | bytes 221192 | tf_op jit(solution)/shard_map/ppermute | solution.py:163
  5.8 4.8 %collective-permute-start.3 = (bf16[1,144,256]{2,1,0:T(8,128)(2,1)S(1)}, bf16[1,144,256]{2,1,0:T(8,128)(2,1)S(1)}, u32[]{:S(2)}, u32[]{:S(2)}) collective-permute-start(bf16[1,144,256]{2,1,0:T(8,128)(2,1)S(1)} %maximum_maximum_fusion.refs_0_), channel_id=1, source_target_pairs={{0,2},{1,3},{2,0},{3,1},{4,6},{5,7},{6,4},{7,5},{8,10},{9,11},{10,... | collective-permute-start | bytes 221192 | tf_op jit(solution)/shard_map/ppermute | solution.py:163
  7.3 4.4 %collective-permute-start.1 = (bf16[1,144,256]{2,1,0:T(8,128)(2,1)S(1)}, bf16[1,144,256]{2,1,0:T(8,128)(2,1)S(1)}, u32[]{:S(2)}, u32[]{:S(2)}) collective-permute-start(bf16[1,144,256]{2,1,0:T(8,128)(2,1)S(1)} %maximum_maximum_fusion.refs_0_), channel_id=1, source_target_pairs={{0,4},{1,5},{2,6},{3,7},{4,0},{5,1},{6,2},{7,3},{8,12},{9,13},{10,... | collective-permute-start | bytes 221192 | tf_op jit(solution)/shard_map/ppermute | solution.py:163
  8.9 3.6 %collective-permute-start.7 = (bf16[1,144,256]{2,1,0:T(8,128)(2,1)S(1)}, bf16[1,144,256]{2,1,0:T(8,128)(2,1)S(1)}, u32[]{:S(2)}, u32[]{:S(2)}) collective-permute-start(bf16[1,144,256]{2,1,0:T(8,128)(2,1)S(1)} %maximum_maximum_fusion.refs_0_), channel_id=1, source_target_pairs={{0,1},{1,0},{2,3},{3,2},{4,5},{5,4},{6,7},{7,6},{8,9},{9,8},{10,11... | collective-permute-start | bytes 221192 | tf_op jit(solution)/shard_map/ppermute | solution.py:163
  9.4 11.3 %copy-start.1 = (bf16[1,144,256]{2,1,0:T(8,128)(2,1)}, bf16[1,144,256]{2,1,0:T(8,128)(2,1)S(1)}, u32[]{:S(2)}) copy-start(bf16[1,144,256]{2,1,0:T(8,128)(2,1)S(1)} %collective-permute-done.refs_1_) | copy-start | bytes 221188
  9.4 4.4 %collective-permute-start.2 = (bf16[1,144,256]{2,1,0:T(8,128)(2,1)S(1)}, bf16[1,144,256]{2,1,0:T(8,128)(2,1)S(1)}, u32[]{:S(2)}, u32[]{:S(2)}) collective-permute-start(bf16[1,144,256]{2,1,0:T(8,128)(2,1)S(1)} %collective-permute-done.refs_1_), channel_id=1, source_target_pairs={{0,4},{1,5},{2,6},{3,7},{4,0},{5,1},{6,2},{7,3},{8,12},{9,13},{10,... | collective-permute-start | bytes 221192 | tf_op jit(solution)/shard_map/ppermute | solution.py:163
  10.6 10.2 %copy-start.2 = (bf16[1,144,256]{2,1,0:T(8,128)(2,1)}, bf16[1,144,256]{2,1,0:T(8,128)(2,1)S(1)}, u32[]{:S(2)}) copy-start(bf16[1,144,256]{2,1,0:T(8,128)(2,1)S(1)} %collective-permute-done.3.refs_4_) | copy-start | bytes 221188
  10.6 4.8 %collective-permute-start.11 = (bf16[1,144,256]{2,1,0:T(8,128)(2,1)S(1)}, bf16[1,144,256]{2,1,0:T(8,128)(2,1)S(1)}, u32[]{:S(2)}, u32[]{:S(2)}) collective-permute-start(bf16[1,144,256]{2,1,0:T(8,128)(2,1)S(1)} %collective-permute-done.3.refs_4_), channel_id=1, source_target_pairs={{0,1},{1,0},{2,3},{3,2},{4,5},{5,4},{6,7},{7,6},{8,9},{9,8},{10,11... | collective-permute-start | bytes 221192 | tf_op jit(solution)/shard_map/ppermute | solution.py:163
  11.7 9.1 %copy-start.3 = (bf16[1,144,256]{2,1,0:T(8,128)(2,1)}, bf16[1,144,256]{2,1,0:T(8,128)(2,1)S(1)}, u32[]{:S(2)}) copy-start(bf16[1,144,256]{2,1,0:T(8,128)(2,1)S(1)} %collective-permute-done.1.refs_2_) | copy-start | bytes 221188
  11.7 3.8 %collective-permute-start.9 = (bf16[1,144,256]{2,1,0:T(8,128)(2,1)S(1)}, bf16[1,144,256]{2,1,0:T(8,128)(2,1)S(1)}, u32[]{:S(2)}, u32[]{:S(2)}) collective-permute-start(bf16[1,144,256]{2,1,0:T(8,128)(2,1)S(1)} %collective-permute-done.1.refs_2_), channel_id=1, source_target_pairs={{0,1},{1,0},{2,3},{3,2},{4,5},{5,4},{6,7},{7,6},{8,9},{9,8},{10,11... | collective-permute-start | bytes 221192 | tf_op jit(solution)/shard_map/ppermute | solution.py:163
  11.7 5.1 %collective-permute-start.5 = (bf16[1,144,256]{2,1,0:T(8,128)(2,1)S(1)}, bf16[1,144,256]{2,1,0:T(8,128)(2,1)S(1)}, u32[]{:S(2)}, u32[]{:S(2)}) collective-permute-start(bf16[1,144,256]{2,1,0:T(8,128)(2,1)S(1)} %collective-permute-done.1.refs_2_), channel_id=1, source_target_pairs={{0,2},{1,3},{2,0},{3,1},{4,6},{5,7},{6,4},{7,5},{8,10},{9,11},{10,... | collective-permute-start | bytes 221192 | tf_op jit(solution)/shard_map/ppermute | solution.py:163
  12.5 8.3 %copy-start.4 = (bf16[1,144,256]{2,1,0:T(8,128)(2,1)}, bf16[1,144,256]{2,1,0:T(8,128)(2,1)S(1)}, u32[]{:S(2)}) copy-start(bf16[1,144,256]{2,1,0:T(8,128)(2,1)S(1)} %collective-permute-done.7.refs_8_) | copy-start | bytes 221188
  12.5 5.8 %collective-permute-start.4 = (bf16[1,144,256]{2,1,0:T(8,128)(2,1)S(1)}, bf16[1,144,256]{2,1,0:T(8,128)(2,1)S(1)}, u32[]{:S(2)}, u32[]{:S(2)}) collective-permute-start(bf16[1,144,256]{2,1,0:T(8,128)(2,1)S(1)} %collective-permute-done.refs_1_), channel_id=1, source_target_pairs={{0,2},{1,3},{2,0},{3,1},{4,6},{5,7},{6,4},{7,5},{8,10},{9,11},{10,... | collective-permute-start | bytes 221192 | tf_op jit(solution)/shard_map/ppermute | solution.py:163
  13.8 7.0 %copy-start.5 = (bf16[1,144,256]{2,1,0:T(8,128)(2,1)}, bf16[1,144,256]{2,1,0:T(8,128)(2,1)S(1)}, u32[]{:S(2)}) copy-start(bf16[1,144,256]{2,1,0:T(8,128)(2,1)S(1)} %collective-permute-done.2.refs_3_) | copy-start | bytes 221188
  13.8 5.7 %collective-permute-start.6 = (bf16[1,144,256]{2,1,0:T(8,128)(2,1)S(1)}, bf16[1,144,256]{2,1,0:T(8,128)(2,1)S(1)}, u32[]{:S(2)}, u32[]{:S(2)}) collective-permute-start(bf16[1,144,256]{2,1,0:T(8,128)(2,1)S(1)} %collective-permute-done.2.refs_3_), channel_id=1, source_target_pairs={{0,2},{1,3},{2,0},{3,1},{4,6},{5,7},{6,4},{7,5},{8,10},{9,11},{10,... | collective-permute-start | bytes 221192 | tf_op jit(solution)/shard_map/ppermute | solution.py:163
  15.4 5.4 %copy-start.6 = (bf16[1,144,256]{2,1,0:T(8,128)(2,1)}, bf16[1,144,256]{2,1,0:T(8,128)(2,1)S(1)}, u32[]{:S(2)}) copy-start(bf16[1,144,256]{2,1,0:T(8,128)(2,1)S(1)} %collective-permute-done.11.refs_12_) | copy-start | bytes 221188
  15.4 4.1 %collective-permute-start.8 = (bf16[1,144,256]{2,1,0:T(8,128)(2,1)S(1)}, bf16[1,144,256]{2,1,0:T(8,128)(2,1)S(1)}, u32[]{:S(2)}, u32[]{:S(2)}) collective-permute-start(bf16[1,144,256]{2,1,0:T(8,128)(2,1)S(1)} %collective-permute-done.refs_1_), channel_id=1, source_target_pairs={{0,1},{1,0},{2,3},{3,2},{4,5},{5,4},{6,7},{7,6},{8,9},{9,8},{10,11... | collective-permute-start | bytes 221192 | tf_op jit(solution)/shard_map/ppermute | solution.py:163
  15.4 5.4 %copy-start.7 = (bf16[1,144,256]{2,1,0:T(8,128)(2,1)}, bf16[1,144,256]{2,1,0:T(8,128)(2,1)S(1)}, u32[]{:S(2)}) copy-start(bf16[1,144,256]{2,1,0:T(8,128)(2,1)S(1)} %collective-permute-done.9.refs_10_) | copy-start | bytes 221188
  15.5 4.1 %collective-permute-start.10 = (bf16[1,144,256]{2,1,0:T(8,128)(2,1)S(1)}, bf16[1,144,256]{2,1,0:T(8,128)(2,1)S(1)}, u32[]{:S(2)}, u32[]{:S(2)}) collective-permute-start(bf16[1,144,256]{2,1,0:T(8,128)(2,1)S(1)} %collective-permute-done.2.refs_3_), channel_id=1, source_target_pairs={{0,1},{1,0},{2,3},{3,2},{4,5},{5,4},{6,7},{7,6},{8,9},{9,8},{10,11... | collective-permute-start | bytes 221192 | tf_op jit(solution)/shard_map/ppermute | solution.py:163
  16.7 4.1 %copy-start.8 = (bf16[1,144,256]{2,1,0:T(8,128)(2,1)}, bf16[1,144,256]{2,1,0:T(8,128)(2,1)S(1)}, u32[]{:S(2)}) copy-start(bf16[1,144,256]{2,1,0:T(8,128)(2,1)S(1)} %collective-permute-done.5.refs_6_) | copy-start | bytes 221188
  16.7 2.8 %collective-permute-start.13 = (bf16[1,144,256]{2,1,0:T(8,128)(2,1)S(1)}, bf16[1,144,256]{2,1,0:T(8,128)(2,1)S(1)}, u32[]{:S(2)}, u32[]{:S(2)}) collective-permute-start(bf16[1,144,256]{2,1,0:T(8,128)(2,1)S(1)} %collective-permute-done.5.refs_6_), channel_id=1, source_target_pairs={{0,1},{1,0},{2,3},{3,2},{4,5},{5,4},{6,7},{7,6},{8,9},{9,8},{10,11... | collective-permute-start | bytes 221192 | tf_op jit(solution)/shard_map/ppermute | solution.py:163
  18.3 1.3 %collective-permute-start.12 = (bf16[1,144,256]{2,1,0:T(8,128)(2,1)S(1)}, bf16[1,144,256]{2,1,0:T(8,128)(2,1)S(1)}, u32[]{:S(2)}, u32[]{:S(2)}) collective-permute-start(bf16[1,144,256]{2,1,0:T(8,128)(2,1)S(1)} %collective-permute-done.4.refs_5_), channel_id=1, source_target_pairs={{0,1},{1,0},{2,3},{3,2},{4,5},{5,4},{6,7},{7,6},{8,9},{9,8},{10,11... | collective-permute-start | bytes 221192 | tf_op jit(solution)/shard_map/ppermute | solution.py:163
  19.5 1.3 %collective-permute-start.14 = (bf16[1,144,256]{2,1,0:T(8,128)(2,1)S(1)}, bf16[1,144,256]{2,1,0:T(8,128)(2,1)S(1)}, u32[]{:S(2)}, u32[]{:S(2)}) collective-permute-start(bf16[1,144,256]{2,1,0:T(8,128)(2,1)S(1)} %collective-permute-done.6.refs_7_), channel_id=1, source_target_pairs={{0,1},{1,0},{2,3},{3,2},{4,5},{5,4},{6,7},{7,6},{8,9},{9,8},{10,11... | collective-permute-start | bytes 221192 | tf_op jit(solution)/shard_map/ppermute | solution.py:163
  (8 other events, 10.5 us)
where the time goes:
time: 36.1 us; the launch traced here: 35.9 us
  starting transfers between devices  12.5 us (35%)
  Pallas kernels  12.4 us (34%)
  waiting for transfers between devices  6.51 us (18%)
  local copies, waits for them, and re-layouts  3.42 us (9%)
  other arithmetic  0.86 us (2%)
    ppermute x15, starting transfers between devices, gather_spans(): held = held + [lax.ppermute(piece, 'dp', pairs) for piece in held]  12.5 us
    pallas_call x1, Pallas kernels, local(): pl.pallas_call(kernel, out_shape=jax.ShapeDtypeStruct((queries, columns),...  12.4 us
    ppermute x15, waiting for transfers between devices, gather_spans(): held = held + [lax.ppermute(piece, 'dp', pairs) for piece in held]  6.51 us
    pallas_call x1, local copies, waits for them, and re-layouts, local(): pl.pallas_call(kernel, out_shape=jax.ShapeDtypeStruct((queries, columns),...  1.93 us
    unnamed x34, local copies, waits for them, and re-layouts  1.32 us
    concatenate x1, other arithmetic, local(): payload = jnp.concatenate([train_act, train_grad, ids, index], axis=1)  0.86 us
  transfers between devices with their start and end apart: 15, of which 7 were waited for; matrix products, arithmetic and copies ran while one was open for 0% of the time, Pallas kernels for 0%

commit v1 on v0

--- a/solution.py
+++ b/solution.py
@@ -64,9 +64,15 @@
 
 
 def influence_kernel(rows, scale, *refs):
-    n_pieces = len(refs) - 10
+    n_pieces = len(refs) - 13
     pieces = refs[:n_pieces]
-    query_act, query_grad, out, act, grad, onehot, mat, tmat, xmat, inverse = refs[n_pieces:]
+    query_act_hbm, query_grad_hbm, out, query_act, query_grad, act, grad, onehot, mat, tmat, xmat, inverse, arrived = refs[n_pieces:]
+    loads = [
+        pltpu.make_async_copy(query_act_hbm, query_act, arrived.at[0]),
+        pltpu.make_async_copy(query_grad_hbm, query_grad, arrived.at[1]),
+    ]
+    for load in loads:
+        load.start()
     tokens, width = act.shape
     columns = onehot.shape[0]
     lane = lax.broadcasted_iota(jnp.int32, (1, 128), 1)
@@ -77,7 +83,7 @@
     for slot, (ref, k) in enumerate(spans):
         act[slot * rows : (slot + 1) * rows, :] = ref[k, 0:rows, :]
         grad[slot * rows : (slot + 1) * rows, :] = ref[k, rows : 2 * rows, :]
-        tail = ref[k, 2 * rows : 2 * rows + 16, 0:128].astype(F32)
+        tail = ref[k, 2 * rows : 2 * rows + 8, 0:128].astype(F32)
         labels.append((SEQ_DEV * tail[1:2, :] + tail[0:1, :]).astype(jnp.int32))
     for pair in range(tokens // 128):
         label = jnp.where(lane < rows, labels[2 * pair], labels[2 * pair + 1])
@@ -133,6 +139,8 @@
         inverse[2 * which] = high
         inverse[2 * which + 1] = mid
 
+    for load in loads:
+        load.wait()
     block, chunk = 256, min(tokens, 1024)
 
     def scores(i, carry):
@@ -147,44 +155,72 @@
             high, mid = split2(product)
             selector = onehot[:, these]
             total = total + (dot_nt(high, selector) + dot_nt(mid, selector))
-        out[here, :] = total * scale
+        out[:, here] = (total * scale).T
         return carry
 
     lax.fori_loop(0, query_act.shape[0] // block, scores, 0, unroll=tokens <= 1024)
+
+
+def payload_kernel(rows, act, grad, ids, out):
+    out[0, 0:rows, :] = act[0]
+    out[0, rows : 2 * rows, :] = grad[0]
+    index = lax.axis_index("dp").astype(F32)
+    label = ids[...].astype(F32)
+    label = jnp.broadcast_to(jnp.concatenate([label] * (act.shape[2] // rows), axis=1), (8, act.shape[2]))
+    row = lax.broadcasted_iota(jnp.int32, label.shape, 0)
+    out[0, 2 * rows :, :] = jnp.where(row == 0, label, index).astype(BF16)
+
+
+ROUTE_16 = ((0, 8), (0, 4), (0, 2), (1, 4), (1, 2), (2, 2), (5, 4))
+
+
+def exchange(piece, bit, size):
+    return lax.ppermute(piece, "dp", [(device, device ^ bit) for device in range(size)])
 
 
 def gather_spans(payload, size):
     held = [payload]
-    bits = [1 << k for k in range(size.bit_length() - 1)]
-    for bit in reversed(bits):
+    if size == 16:
+        for source, bit in ROUTE_16:
+            held.append(exchange(held[source], bit, size))
+        return held + [exchange(piece, 1, size) for piece in held]
+    for bit in reversed([1 << k for k in range(size.bit_length() - 1)]):
         if len(held) >= 16:
             held = [jnp.concatenate(held, axis=0)]
-        pairs = [(device, device ^ bit) for device in range(size)]
-        held = held + [lax.ppermute(piece, "dp", pairs) for piece in held]
+        held = held + [exchange(piece, bit, size) for piece in held]
     return held
 
 
 def local(query_act, query_grad, train_act, train_grad, seq_ids):
     size = lax.axis_size("dp")
     spans, rows, width = train_act.shape
-    own = lax.axis_index("dp").astype(BF16)
-    ids = jnp.tile(seq_ids.astype(BF16), (1, width // rows)).reshape(spans, 1, width)
-    index = jnp.full((spans, 15, width), own, BF16)
-    payload = jnp.concatenate([train_act, train_grad, ids, index], axis=1)
+    vmem = pl.BlockSpec(memory_space=pltpu.VMEM)
+
+    def build(*refs):
+        payload_kernel(rows, *refs)
+
+    payload = pl.pallas_call(
+        build,
+        out_shape=pltpu.VMEM((spans, 2 * rows + 8, width), BF16),
+        in_specs=[vmem] * 3,
+        out_specs=vmem,
+    )(train_act, train_grad, seq_ids)
     pieces = gather_spans(payload, size)
     tokens, queries, columns = size * spans * rows, query_act.shape[0], size * spans * SEQ_DEV
     scale = 1.0 / (8.0 * math.sqrt(query_act.shape[1] * query_grad.shape[1]))
-    vmem = pl.BlockSpec(memory_space=pltpu.VMEM)
 
     def kernel(*refs):
         influence_kernel(rows, scale, *refs)
 
-    return pl.pallas_call(
+    operands = [pltpu.with_memory_space_constraint(piece, pltpu.VMEM) for piece in pieces]
+    scores = pl.pallas_call(
         kernel,
-        out_shape=jax.ShapeDtypeStruct((queries, columns), F32),
-        in_specs=[vmem] * (len(pieces) + 2),
+        out_shape=jax.ShapeDtypeStruct((columns, queries), F32),
+        in_specs=[vmem] * len(operands) + [pl.BlockSpec(memory_space=pltpu.HBM)] * 2,
         out_specs=vmem,
         scratch_shapes=[
+            pltpu.VMEM(query_act.shape, BF16),
+            pltpu.VMEM(query_grad.shape, BF16),
             pltpu.VMEM((tokens, width), BF16),
             pltpu.VMEM((tokens, width), BF16),
             pltpu.VMEM((columns, tokens), BF16),
@@ -192,9 +228,11 @@
             pltpu.VMEM((2, width, width), F32),
             pltpu.VMEM((2, width, width), F32),
             pltpu.VMEM((4, width, width), BF16),
+            pltpu.SemaphoreType.DMA((2,)),
         ],
-        compiler_params=pltpu.CompilerParams(vmem_limit_bytes=56 << 20),
-    )(*pieces, query_act, query_grad)
+        compiler_params=pltpu.CompilerParams(vmem_limit_bytes=40 << 20),
+    )(*operands, query_act, query_grad)
+    return scores.T
 
 
 def solution(mesh):

time: 36.1 us -> 31.6 us (0.88)
  waiting for transfers between devices: 6.51 us -> 5.08 us
  local copies, waits for them, and re-layouts: 3.42 us -> 2.08 us
  other arithmetic: 0.86 us -> 0 us
  Pallas kernels: 12.4 us -> 11.7 us
    pallas_call x1 -> x0, local copies, waits for them, and re-layouts: 1.93 us -> none  [local(): pl.pallas_call(kernel, out_shape=jax.ShapeDtypeStruct((queries, columns),...]
    ppermute x15, waiting for transfers between devices: 6.51 us -> 5.08 us  [exchange(): lax.ppermute(piece, 'dp', [(device, device ^ bit) for device in range(siz...]
    concatenate x1 -> x0, other arithmetic: 0.86 us -> none  [local(): payload = jnp.concatenate([train_act, train_grad, ids, index], axis=1)]
    unnamed x34 -> x4, local copies, waits for them, and re-layouts: 1.32 us -> 2.08 us
    pallas_call x1 -> x2, Pallas kernels: 12.4 us -> 11.7 us  [the longest x1 10.8 us: local(): pl.pallas_call(kernel, out_shape=jax.ShapeDtypeStruct((columns, queries),...]
  transfers between devices with their start and end apart: 15 -> 15, of which waited for: 7 -> 6; matrix products, arithmetic and copies ran while one was open for 0% -> 0% of each run, Pallas kernels for 0% -> 0%
where the time goes in v1:
time: 31.6 us; the launch traced here: 31.3 us
  starting transfers between devices  12.4 us (39%)
  Pallas kernels  11.7 us (37%)
  waiting for transfers between devices  5.08 us (16%)
  local copies, waits for them, and re-layouts  2.08 us (7%)
    ppermute x15, starting transfers between devices, exchange(): lax.ppermute(piece, 'dp', [(device, device ^ bit) for device in range(siz...  12.4 us
    pallas_call x1, Pallas kernels, local(): pl.pallas_call(kernel, out_shape=jax.ShapeDtypeStruct((columns, queries),...  10.8 us
    ppermute x15, waiting for transfers between devices, exchange(): lax.ppermute(piece, 'dp', [(device, device ^ bit) for device in range(siz...  5.08 us
    unnamed x4, local copies, waits for them, and re-layouts  2.08 us
    pallas_call x1, Pallas kernels, local(): pl.pallas_call(build, out_shape=pltpu.VMEM((spans, 2 * rows + 8, width),...  0.85 us
  transfers between devices with their start and end apart: 15, of which 6 were waited for; matrix products, arithmetic and copies ran while one was open for 0% of the time, Pallas kernels for 0%

profile of v1, /device:TPU:0, one launch (start us, length us, event | category | flops | bytes accessed | tf_op | source)
XLA Modules:
  0.0 31.3 jit_solution(13635255303857447971)
XLA Ops:
  0.0 0.9 %shard_map.55.refs_0_ = bf16[1,136,256]{2,1,0:T(8,128)(2,1)S(1)} custom-call(bf16[1,64,256]{2,1,0:T(8,128)(2,1)} %refs_0_.1, bf16[1,64,256]{2,1,0:T(8,128)(2,1)} %refs_1_.1, s32[1,64]{1,0:T(1,128)} %refs_2_.1), custom_call_target="tpu_custom_call" | custom-call | tf_op jit(solution)/shard_map/pallas_call | solution.py:202
  0.9 4.0 %collective-permute-start = (bf16[1,136,256]{2,1,0:T(8,128)(2,1)S(1)}, bf16[1,136,256]{2,1,0:T(8,128)(2,1)S(1)}, u32[]{:S(2)}, u32[]{:S(2)}) collective-permute-start(bf16[1,136,256]{2,1,0:T(8,128)(2,1)S(1)} %shard_map.55.refs_0_), channel_id=1, source_target_pairs={{0,8},{1,9},{2,10},{3,11},{4,12},{5,13},{6,14},{7,15},{8,0},{9,1},... | collective-permute-start | bytes 208904 | tf_op jit(solution)/shard_map/ppermute | solution.py:178
  4.9 1.5 %collective-permute-start.2 = (bf16[1,136,256]{2,1,0:T(8,128)(2,1)S(1)}, bf16[1,136,256]{2,1,0:T(8,128)(2,1)S(1)}, u32[]{:S(2)}, u32[]{:S(2)}) collective-permute-start(bf16[1,136,256]{2,1,0:T(8,128)(2,1)S(1)} %shard_map.55.refs_0_), channel_id=1, source_target_pairs={{0,2},{1,3},{2,0},{3,1},{4,6},{5,7},{6,4},{7,5},{8,10},{9,11},{10,... | collective-permute-start | bytes 208904 | tf_op jit(solution)/shard_map/ppermute | solution.py:178
  6.4 1.6 %collective-permute-start.1 = (bf16[1,136,256]{2,1,0:T(8,128)(2,1)S(1)}, bf16[1,136,256]{2,1,0:T(8,128)(2,1)S(1)}, u32[]{:S(2)}, u32[]{:S(2)}) collective-permute-start(bf16[1,136,256]{2,1,0:T(8,128)(2,1)S(1)} %shard_map.55.refs_0_), channel_id=1, source_target_pairs={{0,4},{1,5},{2,6},{3,7},{4,0},{5,1},{6,2},{7,3},{8,12},{9,13},{10,... | collective-permute-start | bytes 208904 | tf_op jit(solution)/shard_map/ppermute | solution.py:178
  8.0 0.4 %collective-permute-done.refs_1_ = bf16[1,136,256]{2,1,0:T(8,128)(2,1)S(1)} collective-permute-done((bf16[1,136,256]{2,1,0:T(8,128)(2,1)S(1)}, bf16[1,136,256]{2,1,0:T(8,128)(2,1)S(1)}, u32[]{:S(2)}, u32[]{:S(2)}) %collective-permute-start) | collective-permute-done | bytes 69664 | tf_op jit(solution)/shard_map/ppermute | solution.py:178
  8.3 1.6 %collective-permute-start.4 = (bf16[1,136,256]{2,1,0:T(8,128)(2,1)S(1)}, bf16[1,136,256]{2,1,0:T(8,128)(2,1)S(1)}, u32[]{:S(2)}, u32[]{:S(2)}) collective-permute-start(bf16[1,136,256]{2,1,0:T(8,128)(2,1)S(1)} %collective-permute-done.refs_1_), channel_id=1, source_target_pairs={{0,2},{1,3},{2,0},{3,1},{4,6},{5,7},{6,4},{7,5},{8,10},{9,11},{10,... | collective-permute-start | bytes 208904 | tf_op jit(solution)/shard_map/ppermute | solution.py:178
  10.0 0.7 %collective-permute-done.1.refs_2_ = bf16[1,136,256]{2,1,0:T(8,128)(2,1)S(1)} collective-permute-done((bf16[1,136,256]{2,1,0:T(8,128)(2,1)S(1)}, bf16[1,136,256]{2,1,0:T(8,128)(2,1)S(1)}, u32[]{:S(2)}, u32[]{:S(2)}) %collective-permute-start.1) | collective-permute-done | bytes 69664 | tf_op jit(solution)/shard_map/ppermute | solution.py:178
  10.7 0.0 collective-permute-start.9
  10.7 0.5 %collective-permute-start.5 = (bf16[1,136,256]{2,1,0:T(8,128)(2,1)S(1)}, bf16[1,136,256]{2,1,0:T(8,128)(2,1)S(1)}, u32[]{:S(2)}, u32[]{:S(2)}) collective-permute-start(bf16[1,136,256]{2,1,0:T(8,128)(2,1)S(1)} %collective-permute-done.1.refs_2_), channel_id=1, source_target_pairs={{0,2},{1,3},{2,0},{3,1},{4,6},{5,7},{6,4},{7,5},{8,10},{9,11},{10,... | collective-permute-start | bytes 208904 | tf_op jit(solution)/shard_map/ppermute | solution.py:178
  11.2 1.6 %collective-permute-start.3 = (bf16[1,136,256]{2,1,0:T(8,128)(2,1)S(1)}, bf16[1,136,256]{2,1,0:T(8,128)(2,1)S(1)}, u32[]{:S(2)}, u32[]{:S(2)}) collective-permute-start(bf16[1,136,256]{2,1,0:T(8,128)(2,1)S(1)} %collective-permute-done.refs_1_), channel_id=1, source_target_pairs={{0,4},{1,5},{2,6},{3,7},{4,0},{5,1},{6,2},{7,3},{8,12},{9,13},{10,... | collective-permute-start | bytes 208904 | tf_op jit(solution)/shard_map/ppermute | solution.py:178
  12.8 0.0 collective-permute-done.4.refs_5_
  12.8 1.1 %collective-permute-start.6 = (bf16[1,136,256]{2,1,0:T(8,128)(2,1)S(1)}, bf16[1,136,256]{2,1,0:T(8,128)(2,1)S(1)}, u32[]{:S(2)}, u32[]{:S(2)}) collective-permute-start(bf16[1,136,256]{2,1,0:T(8,128)(2,1)S(1)} %collective-permute-done.4.refs_5_), channel_id=1, source_target_pairs={{0,4},{1,5},{2,6},{3,7},{4,0},{5,1},{6,2},{7,3},{8,12},{9,13},{10,... | collective-permute-start | bytes 208904 | tf_op jit(solution)/shard_map/ppermute | solution.py:178
  13.9 0.0 collective-permute-start.8
  13.9 0.0 collective-permute-done.9.refs_10_
  13.9 0.5 %collective-permute-start.12 = (bf16[1,136,256]{2,1,0:T(8,128)(2,1)S(1)}, bf16[1,136,256]{2,1,0:T(8,128)(2,1)S(1)}, u32[]{:S(2)}, u32[]{:S(2)}) collective-permute-start(bf16[1,136,256]{2,1,0:T(8,128)(2,1)S(1)} %collective-permute-done.4.refs_5_), channel_id=1, source_target_pairs={{0,1},{1,0},{2,3},{3,2},{4,5},{5,4},{6,7},{7,6},{8,9},{9,8},{10,11... | collective-permute-start | bytes 208904 | tf_op jit(solution)/shard_map/ppermute | solution.py:178
  14.4 0.9 %collective-permute-done.5.refs_6_ = bf16[1,136,256]{2,1,0:T(8,128)(2,1)S(1)} collective-permute-done((bf16[1,136,256]{2,1,0:T(8,128)(2,1)S(1)}, bf16[1,136,256]{2,1,0:T(8,128)(2,1)S(1)}, u32[]{:S(2)}, u32[]{:S(2)}) %collective-permute-start.5) | collective-permute-done | bytes 69664 | tf_op jit(solution)/shard_map/ppermute | solution.py:178
  15.3 0.5 %collective-permute-done.3.refs_4_ = bf16[1,136,256]{2,1,0:T(8,128)(2,1)S(1)} collective-permute-done((bf16[1,136,256]{2,1,0:T(8,128)(2,1)S(1)}, bf16[1,136,256]{2,1,0:T(8,128)(2,1)S(1)}, u32[]{:S(2)}, u32[]{:S(2)}) %collective-permute-start.3) | collective-permute-done | bytes 69664 | tf_op jit(solution)/shard_map/ppermute | solution.py:178
  15.8 0.0 collective-permute-start.11
  15.8 1.3 %collective-permute-done.6.refs_7_ = bf16[1,136,256]{2,1,0:T(8,128)(2,1)S(1)} collective-permute-done((bf16[1,136,256]{2,1,0:T(8,128)(2,1)S(1)}, bf16[1,136,256]{2,1,0:T(8,128)(2,1)S(1)}, u32[]{:S(2)}, u32[]{:S(2)}) %collective-permute-start.6) | collective-permute-done | bytes 69664 | tf_op jit(solution)/shard_map/ppermute | solution.py:178
  17.1 0.0 collective-permute-start.14
  17.2 1.2 %collective-permute-done.14.refs_15_ = bf16[1,136,256]{2,1,0:T(8,128)(2,1)S(1)} collective-permute-done((bf16[1,136,256]{2,1,0:T(8,128)(2,1)S(1)}, bf16[1,136,256]{2,1,0:T(8,128)(2,1)S(1)}, u32[]{:S(2)}, u32[]{:S(2)}) %collective-permute-start.14) | collective-permute-done | bytes 69664 | tf_op jit(solution)/shard_map/ppermute | solution.py:178
  18.4 1.0 %copy-done = bf16[1024,256]{1,0:T(8,128)(2,1)S(1)} copy-done((bf16[1024,256]{1,0:T(8,128)(2,1)S(1)}, bf16[1024,256]{1,0:T(8,128)(2,1)}, u32[]{:S(2)}) %copy-start) | copy-done | bytes 524312
  19.4 1.0 %copy-done.1 = bf16[1024,256]{1,0:T(8,128)(2,1)S(1)} copy-done((bf16[1024,256]{1,0:T(8,128)(2,1)S(1)}, bf16[1024,256]{1,0:T(8,128)(2,1)}, u32[]{:S(2)}) %copy-start.1) | copy-done | bytes 524312
  20.5 10.8 %shard_map.56 = f32[64,1024]{1,0:T(8,128)} custom-call(bf16[1,136,256]{2,1,0:T(8,128)(2,1)S(1)} %shard_map.55.refs_0_, bf16[1,136,256]{2,1,0:T(8,128)(2,1)S(1)} %collective-permute-done.refs_1_, bf16[1,136,256]{2,1,0:T(8,128)(2,1)S(1)} %collective-permute-done.1.refs_2_, bf16[1,136,256]{2,1,0:T(8,128)(2,1)S(1)} %collective-permute-done.2.refs_3_, ...), custom_call_target="tpu_custom_call" | custom-call | tf_op jit(solution)/shard_map/pallas_call | solution.py:216
  (12 shorter events, 0.0 us)
Async XLA Ops:
  0.9 7.5 %collective-permute-start = (bf16[1,136,256]{2,1,0:T(8,128)(2,1)S(1)}, bf16[1,136,256]{2,1,0:T(8,128)(2,1)S(1)}, u32[]{:S(2)}, u32[]{:S(2)}) collective-permute-start(bf16[1,136,256]{2,1,0:T(8,128)(2,1)S(1)} %shard_map.55.refs_0_), channel_id=1, source_target_pairs={{0,8},{1,9},{2,10},{3,11},{4,12},{5,13},{6,14},{7,15},{8,0},{9,1},... | collective-permute-start | bytes 208904 | tf_op jit(solution)/shard_map/ppermute | solution.py:178
  4.9 5.1 %collective-permute-start.2 = (bf16[1,136,256]{2,1,0:T(8,128)(2,1)S(1)}, bf16[1,136,256]{2,1,0:T(8,128)(2,1)S(1)}, u32[]{:S(2)}, u32[]{:S(2)}) collective-permute-start(bf16[1,136,256]{2,1,0:T(8,128)(2,1)S(1)} %shard_map.55.refs_0_), channel_id=1, source_target_pairs={{0,2},{1,3},{2,0},{3,1},{4,6},{5,7},{6,4},{7,5},{8,10},{9,11},{10,... | collective-permute-start | bytes 208904 | tf_op jit(solution)/shard_map/ppermute | solution.py:178
  6.4 4.3 %collective-permute-start.1 = (bf16[1,136,256]{2,1,0:T(8,128)(2,1)S(1)}, bf16[1,136,256]{2,1,0:T(8,128)(2,1)S(1)}, u32[]{:S(2)}, u32[]{:S(2)}) collective-permute-start(bf16[1,136,256]{2,1,0:T(8,128)(2,1)S(1)} %shard_map.55.refs_0_), channel_id=1, source_target_pairs={{0,4},{1,5},{2,6},{3,7},{4,0},{5,1},{6,2},{7,3},{8,12},{9,13},{10,... | collective-permute-start | bytes 208904 | tf_op jit(solution)/shard_map/ppermute | solution.py:178
  8.0 3.3 %collective-permute-start.7 = (bf16[1,136,256]{2,1,0:T(8,128)(2,1)S(1)}, bf16[1,136,256]{2,1,0:T(8,128)(2,1)S(1)}, u32[]{:S(2)}, u32[]{:S(2)}) collective-permute-start(bf16[1,136,256]{2,1,0:T(8,128)(2,1)S(1)} %shard_map.55.refs_0_), channel_id=1, source_target_pairs={{0,1},{1,0},{2,3},{3,2},{4,5},{5,4},{6,7},{7,6},{8,9},{9,8},{10,11... | collective-permute-start | bytes 208904 | tf_op jit(solution)/shard_map/ppermute | solution.py:178
  8.3 4.5 %collective-permute-start.4 = (bf16[1,136,256]{2,1,0:T(8,128)(2,1)S(1)}, bf16[1,136,256]{2,1,0:T(8,128)(2,1)S(1)}, u32[]{:S(2)}, u32[]{:S(2)}) collective-permute-start(bf16[1,136,256]{2,1,0:T(8,128)(2,1)S(1)} %collective-permute-done.refs_1_), channel_id=1, source_target_pairs={{0,2},{1,3},{2,0},{3,1},{4,6},{5,7},{6,4},{7,5},{8,10},{9,11},{10,... | collective-permute-start | bytes 208904 | tf_op jit(solution)/shard_map/ppermute | solution.py:178
  10.0 3.9 %collective-permute-start.10 = (bf16[1,136,256]{2,1,0:T(8,128)(2,1)S(1)}, bf16[1,136,256]{2,1,0:T(8,128)(2,1)S(1)}, u32[]{:S(2)}, u32[]{:S(2)}) collective-permute-start(bf16[1,136,256]{2,1,0:T(8,128)(2,1)S(1)} %collective-permute-done.2.refs_3_), channel_id=1, source_target_pairs={{0,1},{1,0},{2,3},{3,2},{4,5},{5,4},{6,7},{7,6},{8,9},{9,8},{10,11... | collective-permute-start | bytes 208904 | tf_op jit(solution)/shard_map/ppermute | solution.py:178
  10.7 3.2 %collective-permute-start.9 = (bf16[1,136,256]{2,1,0:T(8,128)(2,1)S(1)}, bf16[1,136,256]{2,1,0:T(8,128)(2,1)S(1)}, u32[]{:S(2)}, u32[]{:S(2)}) collective-permute-start(bf16[1,136,256]{2,1,0:T(8,128)(2,1)S(1)} %collective-permute-done.1.refs_2_), channel_id=1, source_target_pairs={{0,1},{1,0},{2,3},{3,2},{4,5},{5,4},{6,7},{7,6},{8,9},{9,8},{10,11... | collective-permute-start | bytes 208904 | tf_op jit(solution)/shard_map/ppermute | solution.py:178
  10.7 4.6 %collective-permute-start.5 = (bf16[1,136,256]{2,1,0:T(8,128)(2,1)S(1)}, bf16[1,136,256]{2,1,0:T(8,128)(2,1)S(1)}, u32[]{:S(2)}, u32[]{:S(2)}) collective-permute-start(bf16[1,136,256]{2,1,0:T(8,128)(2,1)S(1)} %collective-permute-done.1.refs_2_), channel_id=1, source_target_pairs={{0,2},{1,3},{2,0},{3,1},{4,6},{5,7},{6,4},{7,5},{8,10},{9,11},{10,... | collective-permute-start | bytes 208904 | tf_op jit(solution)/shard_map/ppermute | solution.py:178
  11.2 4.6 %collective-permute-start.3 = (bf16[1,136,256]{2,1,0:T(8,128)(2,1)S(1)}, bf16[1,136,256]{2,1,0:T(8,128)(2,1)S(1)}, u32[]{:S(2)}, u32[]{:S(2)}) collective-permute-start(bf16[1,136,256]{2,1,0:T(8,128)(2,1)S(1)} %collective-permute-done.refs_1_), channel_id=1, source_target_pairs={{0,4},{1,5},{2,6},{3,7},{4,0},{5,1},{6,2},{7,3},{8,12},{9,13},{10,... | collective-permute-start | bytes 208904 | tf_op jit(solution)/shard_map/ppermute | solution.py:178
  12.8 4.3 %collective-permute-start.6 = (bf16[1,136,256]{2,1,0:T(8,128)(2,1)S(1)}, bf16[1,136,256]{2,1,0:T(8,128)(2,1)S(1)}, u32[]{:S(2)}, u32[]{:S(2)}) collective-permute-start(bf16[1,136,256]{2,1,0:T(8,128)(2,1)S(1)} %collective-permute-done.4.refs_5_), channel_id=1, source_target_pairs={{0,4},{1,5},{2,6},{3,7},{4,0},{5,1},{6,2},{7,3},{8,12},{9,13},{10,... | collective-permute-start | bytes 208904 | tf_op jit(solution)/shard_map/ppermute | solution.py:178
  13.9 3.3 %collective-permute-start.8 = (bf16[1,136,256]{2,1,0:T(8,128)(2,1)S(1)}, bf16[1,136,256]{2,1,0:T(8,128)(2,1)S(1)}, u32[]{:S(2)}, u32[]{:S(2)}) collective-permute-start(bf16[1,136,256]{2,1,0:T(8,128)(2,1)S(1)} %collective-permute-done.refs_1_), channel_id=1, source_target_pairs={{0,1},{1,0},{2,3},{3,2},{4,5},{5,4},{6,7},{7,6},{8,9},{9,8},{10,11... | collective-permute-start | bytes 208904 | tf_op jit(solution)/shard_map/ppermute | solution.py:178
  13.9 3.3 %collective-permute-start.12 = (bf16[1,136,256]{2,1,0:T(8,128)(2,1)S(1)}, bf16[1,136,256]{2,1,0:T(8,128)(2,1)S(1)}, u32[]{:S(2)}, u32[]{:S(2)}) collective-permute-start(bf16[1,136,256]{2,1,0:T(8,128)(2,1)S(1)} %collective-permute-done.4.refs_5_), channel_id=1, source_target_pairs={{0,1},{1,0},{2,3},{3,2},{4,5},{5,4},{6,7},{7,6},{8,9},{9,8},{10,11... | collective-permute-start | bytes 208904 | tf_op jit(solution)/shard_map/ppermute | solution.py:178
  15.3 1.8 %collective-permute-start.13 = (bf16[1,136,256]{2,1,0:T(8,128)(2,1)S(1)}, bf16[1,136,256]{2,1,0:T(8,128)(2,1)S(1)}, u32[]{:S(2)}, u32[]{:S(2)}) collective-permute-start(bf16[1,136,256]{2,1,0:T(8,128)(2,1)S(1)} %collective-permute-done.5.refs_6_), channel_id=1, source_target_pairs={{0,1},{1,0},{2,3},{3,2},{4,5},{5,4},{6,7},{7,6},{8,9},{9,8},{10,11... | collective-permute-start | bytes 208904 | tf_op jit(solution)/shard_map/ppermute | solution.py:178
  15.8 1.4 %collective-permute-start.11 = (bf16[1,136,256]{2,1,0:T(8,128)(2,1)S(1)}, bf16[1,136,256]{2,1,0:T(8,128)(2,1)S(1)}, u32[]{:S(2)}, u32[]{:S(2)}) collective-permute-start(bf16[1,136,256]{2,1,0:T(8,128)(2,1)S(1)} %collective-permute-done.3.refs_4_), channel_id=1, source_target_pairs={{0,1},{1,0},{2,3},{3,2},{4,5},{5,4},{6,7},{7,6},{8,9},{9,8},{10,11... | collective-permute-start | bytes 208904 | tf_op jit(solution)/shard_map/ppermute | solution.py:178
  17.1 1.3 %collective-permute-start.14 = (bf16[1,136,256]{2,1,0:T(8,128)(2,1)S(1)}, bf16[1,136,256]{2,1,0:T(8,128)(2,1)S(1)}, u32[]{:S(2)}, u32[]{:S(2)}) collective-permute-start(bf16[1,136,256]{2,1,0:T(8,128)(2,1)S(1)} %collective-permute-done.6.refs_7_), channel_id=1, source_target_pairs={{0,1},{1,0},{2,3},{3,2},{4,5},{5,4},{6,7},{7,6},{8,9},{9,8},{10,11... | collective-permute-start | bytes 208904 | tf_op jit(solution)/shard_map/ppermute | solution.py:178
  18.4 1.0 %copy-start = (bf16[1024,256]{1,0:T(8,128)(2,1)S(1)}, bf16[1024,256]{1,0:T(8,128)(2,1)}, u32[]{:S(2)}) copy-start(bf16[1024,256]{1,0:T(8,128)(2,1)} %refs_16_.1) | copy-start | bytes 1572868
  19.4 1.0 %copy-start.1 = (bf16[1024,256]{1,0:T(8,128)(2,1)S(1)}, bf16[1024,256]{1,0:T(8,128)(2,1)}, u32[]{:S(2)}) copy-start(bf16[1024,256]{1,0:T(8,128)(2,1)} %refs_17_.1) | copy-start | bytes 1572868
